TPU v7x, 32 devices: a whole 2x2x4 slice. The times are simulated.
32 devices in a mesh: leaf: 8 (over z, y), bond: 4 (over x, core).
Axes of the slice: x: 2, y: 2, z: 4, core: 2. Of those that a mesh axis runs over, the one named last changes fastest.
Arguments:
- leaf_metric: float32 [4, 32, 1024], P('bond', 'leaf'), may hold values from -257 to 257, as said below
- local_iso: float32 [24, 32, 1024], P('leaf', 'bond'), may hold values from -6 to 6
- top_iso: float32 [8, 32, 1024], P('leaf', 'bond'), may hold values from -6 to 6
Outputs:
- leaf_rho: float32 [4, 32, 1024], P('bond', 'leaf')
- inner_rho: float32 [4, 24, 1024], P('bond', 'leaf')
- top_rho: float32 [4, 8, 1024], P('bond', 'leaf')
Inputs may be any that keep to these rules, and one draw needn't show every extreme that they name: Each entry of leaf_metric, taken as a 32 x 32 matrix, is symmetric positive definite.
All inputs are finite; a program needn't handle non-finite values.
Results may differ from a plain program's by a relative error of at most 0.0003.
Values sent between devices are 32-bit elements; how exact they have to be, the bound alone decides.
A program may use at most 64 MiB of HBM per device.

v0:
```python
import functools

import jax
import jax.numpy as jnp
from jax import lax
from jax.experimental import pallas as pl
from jax.experimental.pallas import tpu as pltpu
from jax.sharding import PartitionSpec as P

LANES = 128
MESH = pl.DeviceIdType.MESH
EXACT = lax.Precision.HIGHEST


def mm(a, b):
    return jnp.dot(a, b, precision=EXACT, preferred_element_type=jnp.float32)


def mm_nt(a, b):
    return lax.dot_general(
        a, b, (((1,), (1,)), ((), ())), precision=EXACT, preferred_element_type=jnp.float32
    )


def kernel(
    cfg,
    leaf_ref,
    local_ref,
    top_ref,
    leaf_out,
    inner_out,
    top_out,
    raw,
    loc,
    wc,
    wrep,
    yt,
    fbuf,
    tbuf,
    esend,
    erecv,
    own_sem,
    loc_send,
    loc_recv,
    leaf_send,
    leaf_recv,
    fwd_send,
    fwd_recv,
    env_send,
    env_recv,
):
    chi, leaves, devices, bonds = cfg
    cols = chi * chi
    rep = LANES // chi
    chunks = cols // LANES
    levels = devices.bit_length() - 1
    height_dev = leaves.bit_length() - 1
    nodes = leaves - 1
    first = leaves // 2
    position = lax.axis_index("leaf")
    mine = lax.axis_index("bond")

    leaf_peers = [position ^ (1 << k) for k in range(levels)]
    bond_peers = [lax.rem(mine + r, bonds) for r in range(1, bonds)]

    barrier = pltpu.get_barrier_semaphore()
    for peer in leaf_peers:
        pl.semaphore_signal(barrier, inc=1, device_id=(peer, mine), device_id_type=MESH)
    for peer in bond_peers:
        pl.semaphore_signal(barrier, inc=1, device_id=(position, peer), device_id_type=MESH)
    own = [
        pltpu.make_async_copy(top_ref.at[0], raw.at[mine, position], own_sem.at[0]),
        pltpu.make_async_copy(local_ref, loc.at[mine], own_sem.at[1]),
    ]
    for copy in own:
        copy.start()
    pl.semaphore_wait(barrier, levels + bonds - 1)

    starts = [cols - (cols >> k) for k in range(levels + 1)]
    aligned = [s // LANES * LANES for s in starts]
    sends = []

    def local_copies(part, lo, hi):
        found = []
        for r, peer in enumerate(bond_peers):
            found.append(
                pltpu.make_async_remote_copy(
                    src_ref=local_ref.at[lo:hi],
                    dst_ref=loc.at[mine, lo:hi],
                    send_sem=loc_send.at[part, r],
                    recv_sem=loc_recv.at[part, r],
                    device_id=(position, peer),
                    device_id_type=MESH,
                )
            )
        for copy in found:
            copy.start()
        sends.extend(found)
        return found

    def leaf_copy(k):
        base = (position >> k) << k
        slots = raw.at[mine, pl.ds(base, 1 << k), :, aligned[k] : cols]
        source = slots if k else top_ref
        copy = pltpu.make_async_remote_copy(
            src_ref=source,
            dst_ref=slots,
            send_sem=leaf_send.at[k],
            recv_sem=leaf_recv.at[k],
            device_id=(leaf_peers[k], mine),
            device_id_type=MESH,
        )
        copy.start()
        sends.append(copy)
        return copy

    def forward_copies(k):
        base = (position >> (k + 1)) << (k + 1)
        stop = cols if k == levels - 1 else -(-starts[k + 1] // LANES) * LANES
        found = []
        for r, peer in enumerate(bond_peers):
            slots = raw.at[mine, pl.ds(base, 2 << k), :, aligned[k] : stop]
            found.append(
                pltpu.make_async_remote_copy(
                    src_ref=slots,
                    dst_ref=slots,
                    send_sem=fwd_send.at[k, r],
                    recv_sem=fwd_recv.at[k, r],
                    device_id=(position, peer),
                    device_id_type=MESH,
                )
            )
        for copy in found:
            copy.start()
        sends.extend(found)
        return found

    local_moves = [local_copies(0, 0, first)]
    leaf_moves = [leaf_copy(0)]
    if nodes > first:
        local_moves.append(local_copies(1, first, nodes))
    forward_moves = []
    for copy in own:
        copy.wait()

    def advance():
        k = len(forward_moves)
        if k < levels:
            leaf_moves[k].wait_recv()
            if k + 1 < levels:
                leaf_moves.append(leaf_copy(k + 1))
            forward_moves.append(forward_copies(k))

    row = lax.broadcasted_iota(jnp.int32, (chi, LANES), 0)
    lane = lax.broadcasted_iota(jnp.int32, (chi, LANES), 1)
    group = lane // chi
    row_mask = group == lax.rem(row, rep)
    diag_mask = row == lane
    big_row = lax.broadcasted_iota(jnp.int32, (LANES, LANES), 0)
    big_lane = lax.broadcasted_iota(jnp.int32, (LANES, LANES), 1)
    block_mask = big_row // chi == big_lane // chi
    pick = (
        lax.broadcasted_iota(jnp.int32, (chunks, chi), 1) // rep
        == lax.broadcasted_iota(jnp.int32, (chunks, chi), 0)
    ).astype(jnp.float32)
    spread = (
        lax.broadcasted_iota(jnp.int32, (chi, chunks), 0) // rep
        == lax.broadcasted_iota(jnp.int32, (chi, chunks), 1)
    ).astype(jnp.float32)
    widen = (
        lax.broadcasted_iota(jnp.int32, (chi, cols), 1) // chi
        == lax.broadcasted_iota(jnp.int32, (chi, cols), 0)
    ).astype(jnp.float32)

    def fold(value):
        shift = chi
        while shift < LANES:
            value = value + pltpu.roll(value, shift, 1)
            shift *= 2
        return value

    def normalize(matrix):
        trace = jnp.sum(jnp.where(diag_mask, matrix, 0.0), axis=(0, 1), keepdims=True)
        return matrix * (chi / trace)

    def unflatten(line):
        tile = jnp.concatenate(
            [line[:, g * LANES : (g + 1) * LANES] for g in range(chunks)], axis=0
        )
        return fold(jnp.where(row_mask, mm(spread, tile), 0.0))

    def flatten(matrix, out, index):
        tile = mm(pick, jnp.where(row_mask, matrix, 0.0))
        for g in range(chunks):
            out[0, index : index + 1, g * LANES : (g + 1) * LANES] = tile[g : g + 1]

    def lanes_to_rows(value):
        return jnp.concatenate(
            [value[:, g * LANES : (g + 1) * LANES] for g in range(chunks)], axis=0
        )

    def rows_to_lanes(value):
        return jnp.concatenate([value[g * chi : (g + 1) * chi] for g in range(chunks)], axis=1)

    def swap_children(value):
        for g in range(chunks):
            tbuf[g * LANES : (g + 1) * LANES, :] = value[:, g * LANES : (g + 1) * LANES].T
        pieces = []
        for g in range(chunks):
            block = jnp.concatenate(
                [tbuf[pl.ds(rep * g + i, chi, stride=chi), :] for i in range(rep)], axis=0
            )
            pieces.append(block.T)
        return jnp.concatenate(pieces, axis=1)

    def store(item, value):
        for g in range(chunks):
            chunk = value[:, g * LANES : (g + 1) * LANES]
            wc[item, g * chi : (g + 1) * chi, :] = chunk
            for i in range(rep):
                wrep[item, rep * g + i] = fold(jnp.where(group == i, chunk, 0.0))

    def act_minor(item, env):
        block = jnp.where(block_mask, jnp.concatenate([env] * rep, axis=0), 0.0)
        return rows_to_lanes(mm(wc[item], block))

    def act_major(item, env):
        fbuf[...] = mm(env[:, :chi], widen)

        def step(y, sums):
            line = fbuf[pl.ds(y, 1), :]
            block = wrep[item, y]
            return tuple(
                sums[g] + line[:, g * LANES : (g + 1) * LANES] * block for g in range(chunks)
            )

        zero = jnp.zeros((chi, LANES), jnp.float32)
        sums = lax.fori_loop(0, chi, step, (zero,) * chunks, unroll=4)
        yt[item] = jnp.concatenate(sums, axis=0).T
        return jnp.concatenate(sums, axis=1)

    def close(left, right):
        small = mm_nt(left, right)
        return normalize(jnp.concatenate([small] * rep, axis=1))

    def descend(item, state):
        mixed = mm(state[:, :chi], rows_to_lanes(wc[item]))
        square = jnp.where(block_mask, mm(yt[item], lanes_to_rows(mixed)), 0.0)
        total = square[:chi]
        for i in range(1, rep):
            total = total + square[i * chi : (i + 1) * chi]
        return normalize(fold(total))

    envs = [[unflatten(leaf_ref[0, n : n + 1, :]) for n in range(leaves)]]
    advance()
    for copy in local_moves[0]:
        copy.wait_recv()
    waited = 1
    node = 0
    for height in range(1, height_dev + 1):
        if height == 2:
            for copy in local_moves[1]:
                copy.wait_recv()
        current = envs[-1]
        grown = []
        for n in range(leaves >> height):
            value = jnp.concatenate([loc[j, node] for j in range(bonds)], axis=0)
            store(2 * node, value)
            store(2 * node + 1, swap_children(value))
            left, right = current[2 * n], current[2 * n + 1]
            by_left = act_major(2 * node, left)
            act_major(2 * node + 1, right)
            grown.append(close(act_minor(2 * node, right), by_left))
            node += 1
            advance()
        envs.append(grown)
    while len(forward_moves) < levels:
        advance()

    env = envs[-1][0]

    def assemble(k, start, width):
        count = min(2 << k, devices)
        base = (position >> (k + 1)) << (k + 1)
        rows = []
        for j in range(bonds):
            rows.append(
                jnp.concatenate(
                    [raw[j, base + s, :, start : start + width] for s in range(count)], axis=1
                )
            )
        return jnp.concatenate(rows, axis=0)

    exchanges = []
    for k in range(levels):
        esend[k] = env
        copy = pltpu.make_async_remote_copy(
            src_ref=esend.at[k],
            dst_ref=erecv.at[k],
            send_sem=env_send.at[k],
            recv_sem=env_recv.at[k],
            device_id=(leaf_peers[k], mine),
            device_id_type=MESH,
        )
        copy.start()
        sends.append(copy)
        for move in forward_moves[k]:
            move.wait_recv()
        item = 2 * nodes + k
        value = assemble(k, starts[k], cols >> (k + 1))
        upper = lax.rem(position >> k, 2) == 1
        store(item, jnp.where(upper, value, swap_children(value)))
        minor = act_minor(item, env)
        copy.wait_recv()
        env = close(minor, act_major(item, erecv[k]))

    root = assemble(levels - 1, starts[levels], cols >> levels)
    state = close(root, root)
    top = env
    for k in range(levels - 1, -1, -1):
        marked = lax.rem(position + 1, 2 << k) == 1 << k
        top = jnp.where(marked, state, top)
        state = descend(2 * nodes + k, state)
    flatten(top, top_out, 0)
    states = [state]
    for height in range(height_dev, 0, -1):
        count = leaves >> height
        offset = leaves - 2 * count
        below = []
        for n in range(count):
            node = offset + n
            flatten(states[n], inner_out, node)
            below.append(descend(2 * node + 1, states[n]))
            below.append(descend(2 * node, states[n]))
        states = below
    for n in range(leaves):
        flatten(states[n], leaf_out, n)
    for copy in sends:
        copy.wait_send()


def body(cfg, leaf_metric, local_iso, top_iso):
    chi, leaves, devices, bonds = cfg
    cols = chi * chi
    nodes = leaves - 1
    levels = devices.bit_length() - 1
    share = chi // bonds
    items = 2 * nodes + levels
    f32 = jnp.float32
    dma = pltpu.SemaphoreType.DMA
    vmem = pl.BlockSpec(memory_space=pltpu.VMEM)
    return pl.pallas_call(
        functools.partial(kernel, cfg),
        out_shape=(
            jax.ShapeDtypeStruct((1, leaves, cols), f32),
            jax.ShapeDtypeStruct((1, nodes, cols), f32),
            jax.ShapeDtypeStruct((1, 1, cols), f32),
        ),
        in_specs=[vmem] * 3,
        out_specs=(vmem,) * 3,
        scratch_shapes=[
            pltpu.VMEM((bonds, devices, share, cols), f32),
            pltpu.VMEM((bonds, nodes, share, cols), f32),
            pltpu.VMEM((items, cols * chi // LANES, LANES), f32),
            pltpu.VMEM((items, chi, chi, LANES), f32),
            pltpu.VMEM((items, LANES, cols * chi // LANES), f32),
            pltpu.VMEM((chi, cols), f32),
            pltpu.VMEM((cols, chi), f32),
            pltpu.VMEM((levels, chi, LANES), f32),
            pltpu.VMEM((levels, chi, LANES), f32),
            dma((2,)),
            dma((2, bonds - 1)),
            dma((2, bonds - 1)),
            dma((levels,)),
            dma((levels,)),
            dma((levels, bonds - 1)),
            dma((levels, bonds - 1)),
            dma((levels,)),
            dma((levels,)),
        ],
        compiler_params=pltpu.CompilerParams(collective_id=0, has_side_effects=True),
        name="tree_sweep",
    )(leaf_metric, local_iso, top_iso)


def solution(mesh):
    devices, bonds = mesh.shape["leaf"], mesh.shape["bond"]
    spec = P("bond", "leaf", None)
    iso = P("leaf", "bond", None)

    def whole(leaf_metric, local_iso, top_iso):
        cfg = (local_iso.shape[1], leaf_metric.shape[1] // devices, devices, bonds)
        return jax.shard_map(
            functools.partial(body, cfg),
            mesh=mesh,
            in_specs=(spec, iso, iso),
            out_specs=(spec, spec, spec),
            check_vma=False,
        )(leaf_metric, local_iso, top_iso)

    return whole
```

profile of v0, /device:TPU:0, one launch (start us, length us, event | category | flops | bytes accessed | tf_op | source)
XLA Modules:
  0.0 51.9 jit_solution(2904872822380119665)
XLA Ops:
  0.6 48.7 %tree_sweep.1 = (f32[1,4,1024]{2,1,0:T(4,128)}, f32[1,3,1024]{2,1,0:T(4,128)}, f32[1,1,1024]{2,1,0:T(1,128)}) custom-call(f32[1,4,1024]{2,1,0:T(4,128)} %leaf_ref.1, f32[3,8,1024]{2,1,0:T(8,128)} %local_ref.1, f32[1,8,1024]{2,1,0:T(8,128)} %top_ref.1), custom_call_target="tpu_custom_call" | custom-call | tf_op jit(solution)/shard_map/tree_sweep/pallas_call | solution.py:352
  49.3 0.0 copy-start
  49.3 1.3 %copy.6 = f32[1,3,1024]{2,0,1:T(1,128)} copy(f32[1,3,1024]{2,1,0:T(4,128)} %get-tuple-element.4) | data formatting | bytes 24576 | tf_op jit(solution)/shard_map/tree_sweep/pallas_call | solution.py:352
  50.7 0.0 copy-done
  50.7 0.0 copy-start.1
  50.7 0.6 %copy.9 = f32[1,4,1024]{2,1,0:T(4,128)} copy(f32[1,4,1024]{2,1,0:T(4,128)S(1)} %copy-done) | data formatting | bytes 32768
  51.3 0.1 copy-done.1
  51.3 0.6 %copy.10 = f32[1,1,1024]{2,1,0:T(1,128)} copy(f32[1,1,1024]{2,1,0:T(1,128)S(1)} %copy-done.1) | data formatting | bytes 8192
Async XLA Ops:
  49.3 1.3 %copy-start = (f32[1,4,1024]{2,1,0:T(4,128)S(1)}, f32[1,4,1024]{2,1,0:T(4,128)}, u32[]{:S(2)}) copy-start(f32[1,4,1024]{2,1,0:T(4,128)} %get-tuple-element.9) | copy-start | bytes 49156
  50.7 0.7 %copy-start.1 = (f32[1,1,1024]{2,1,0:T(1,128)S(1)}, f32[1,1,1024]{2,1,0:T(1,128)}, u32[]{:S(2)}) copy-start(f32[1,1,1024]{2,1,0:T(1,128)} %get-tuple-element.11) | copy-start | bytes 12292
where the time goes:
time: 52.2 us; the launch traced here: 51.9 us
  Pallas kernels  48.7 us (93%)
  local copies, waits for them, and re-layouts  2.61 us (5%)
  between operations  0.65 us (1%)
    pallas_call x1, Pallas kernels, body(): pl.pallas_call(functools.partial(kernel, cfg), out_shape=(jax.ShapeDtypeS...  48.7 us
    pallas_call x1, local copies, waits for them, and re-layouts, body(): pl.pallas_call(functools.partial(kernel, cfg), out_shape=(jax.ShapeDtypeS...  1.33 us
    unnamed x6, local copies, waits for them, and re-layouts  1.27 us

commit v1 on v0

--- a/solution.py
+++ b/solution.py
@@ -16,10 +16,27 @@
     return jnp.dot(a, b, precision=EXACT, preferred_element_type=jnp.float32)
 
 
-def mm_nt(a, b):
-    return lax.dot_general(
-        a, b, (((1,), (1,)), ((), ())), precision=EXACT, preferred_element_type=jnp.float32
-    )
+def dot(a, b):
+    return jnp.dot(a, b, preferred_element_type=jnp.float32)
+
+
+def dot_nt(a, b):
+    return lax.dot_general(a, b, (((1,), (1,)), ((), ())), preferred_element_type=jnp.float32)
+
+
+def halves(value):
+    high = value.astype(jnp.bfloat16)
+    low = (value - high.astype(jnp.float32)).astype(jnp.bfloat16)
+    return high, low
+
+
+def join_lanes(value):
+    return value[:, :LANES] + value[:, LANES:]
+
+
+def join_rows(value):
+    half = value.shape[0] // 2
+    return value[:half] + value[half:]
 
 
 def kernel(
@@ -32,7 +49,8 @@
     top_out,
     raw,
     loc,
-    wc,
+    wk,
+    wm,
     wrep,
     yt,
     fbuf,
@@ -168,9 +186,17 @@
         == lax.broadcasted_iota(jnp.int32, (chi, chunks), 1)
     ).astype(jnp.float32)
     widen = (
-        lax.broadcasted_iota(jnp.int32, (chi, cols), 1) // chi
-        == lax.broadcasted_iota(jnp.int32, (chi, cols), 0)
-    ).astype(jnp.float32)
+        lax.broadcasted_iota(jnp.int32, (LANES, cols), 1) // chi
+        == lax.rem(lax.broadcasted_iota(jnp.int32, (LANES, cols), 0), chi)
+    ).astype(jnp.float32).astype(jnp.bfloat16)
+    copy_row = lax.broadcasted_iota(jnp.int32, (2 * LANES, rep * LANES), 0)
+    copy_lane = lax.broadcasted_iota(jnp.int32, (2 * LANES, rep * LANES), 1)
+    copies = jnp.where(
+        (lax.rem(copy_row, LANES) // chi == copy_lane // LANES)
+        & (lax.rem(copy_row, chi) == lax.rem(copy_lane, chi)),
+        1.0,
+        0.0,
+    ).astype(jnp.bfloat16)
 
     def fold(value):
         shift = chi
@@ -214,18 +240,29 @@
         return jnp.concatenate(pieces, axis=1)
 
     def store(item, value):
+        high, low = halves(value)
+        wm[item] = jnp.concatenate([high, low] * (rep // 2), axis=0)
+        stack = jnp.concatenate([lanes_to_rows(high), lanes_to_rows(low)], axis=1)
+        wk[item] = stack
+        spread_out = dot(stack, copies)
         for g in range(chunks):
-            chunk = value[:, g * LANES : (g + 1) * LANES]
-            wc[item, g * chi : (g + 1) * chi, :] = chunk
             for i in range(rep):
-                wrep[item, rep * g + i] = fold(jnp.where(group == i, chunk, 0.0))
+                wrep[item, rep * g + i] = spread_out[
+                    g * chi : (g + 1) * chi, i * LANES : (i + 1) * LANES
+                ]
 
     def act_minor(item, env):
         block = jnp.where(block_mask, jnp.concatenate([env] * rep, axis=0), 0.0)
-        return rows_to_lanes(mm(wc[item], block))
+        pair = jnp.concatenate(halves(block), axis=1)
+        return rows_to_lanes(join_lanes(dot(wk[item], jnp.concatenate([pair, pair], axis=0))))
 
     def act_major(item, env):
-        fbuf[...] = mm(env[:, :chi], widen)
+        high = env.astype(jnp.bfloat16).astype(jnp.float32)
+        rest = env - high
+        middle = rest.astype(jnp.bfloat16).astype(jnp.float32)
+        low = jnp.where(group == 2, rest - middle, 0.0)
+        parts = jnp.where(group == 0, high, jnp.where(group == 1, middle, low))
+        fbuf[...] = dot(parts.astype(jnp.bfloat16), widen)
 
         def step(y, sums):
             line = fbuf[pl.ds(y, 1), :]
@@ -236,16 +273,21 @@
 
         zero = jnp.zeros((chi, LANES), jnp.float32)
         sums = lax.fori_loop(0, chi, step, (zero,) * chunks, unroll=4)
-        yt[item] = jnp.concatenate(sums, axis=0).T
+        yt[item] = jnp.concatenate(halves(jnp.concatenate(sums, axis=0).T), axis=0)
         return jnp.concatenate(sums, axis=1)
 
     def close(left, right):
-        small = mm_nt(left, right)
-        return normalize(jnp.concatenate([small] * rep, axis=1))
+        high, low = halves(right)
+        wide = jnp.concatenate([high] * rep + [low] * rep, axis=0)
+        tall = jnp.concatenate(halves(left), axis=0)
+        return normalize(join_lanes(join_rows(dot_nt(tall, wide))))
 
     def descend(item, state):
-        mixed = mm(state[:, :chi], rows_to_lanes(wc[item]))
-        square = jnp.where(block_mask, mm(yt[item], lanes_to_rows(mixed)), 0.0)
+        high = state.astype(jnp.bfloat16).astype(jnp.float32)
+        parts = jnp.where(group < rep // 2, high, state - high).astype(jnp.bfloat16)
+        mixed = lanes_to_rows(dot(parts, wm[item]))
+        square = dot(yt[item], jnp.concatenate(halves(mixed), axis=1))
+        square = jnp.where(block_mask, join_lanes(join_rows(square)), 0.0)
         total = square[:chi]
         for i in range(1, rep):
             total = total + square[i * chi : (i + 1) * chi]
@@ -270,7 +312,7 @@
             left, right = current[2 * n], current[2 * n + 1]
             by_left = act_major(2 * node, left)
             act_major(2 * node + 1, right)
-            grown.append(close(act_minor(2 * node, right), by_left))
+            grown.append(close(by_left, act_minor(2 * node, right)))
             node += 1
             advance()
         envs.append(grown)
@@ -312,7 +354,7 @@
         store(item, jnp.where(upper, value, swap_children(value)))
         minor = act_minor(item, env)
         copy.wait_recv()
-        env = close(minor, act_major(item, erecv[k]))
+        env = close(act_major(item, erecv[k]), minor)
 
     root = assemble(levels - 1, starts[levels], cols >> levels)
     state = close(root, root)
@@ -361,9 +403,10 @@
         scratch_shapes=[
             pltpu.VMEM((bonds, devices, share, cols), f32),
             pltpu.VMEM((bonds, nodes, share, cols), f32),
-            pltpu.VMEM((items, cols * chi // LANES, LANES), f32),
+            pltpu.VMEM((items, cols * chi // LANES, 2 * LANES), jnp.bfloat16),
+            pltpu.VMEM((items, LANES, cols), jnp.bfloat16),
             pltpu.VMEM((items, chi, chi, LANES), f32),
-            pltpu.VMEM((items, LANES, cols * chi // LANES), f32),
+            pltpu.VMEM((items, 2 * LANES, cols * chi // LANES), jnp.bfloat16),
             pltpu.VMEM((chi, cols), f32),
             pltpu.VMEM((cols, chi), f32),
             pltpu.VMEM((levels, chi, LANES), f32),

time: 52.2 us -> 39.4 us (0.75)
  Pallas kernels: 48.7 us -> 35.9 us
    pallas_call x1, Pallas kernels: 48.7 us -> 35.9 us  [body(): pl.pallas_call(functools.partial(kernel, cfg), out_shape=(jax.ShapeDtypeS...]
where the time goes in v1:
time: 39.4 us; the launch traced here: 39.1 us
  Pallas kernels  35.9 us (91%)
  local copies, waits for them, and re-layouts  2.61 us (7%)
  between operations  0.65 us (2%)
    pallas_call x1, Pallas kernels, body(): pl.pallas_call(functools.partial(kernel, cfg), out_shape=(jax.ShapeDtypeS...  35.9 us
    pallas_call x1, local copies, waits for them, and re-layouts, body(): pl.pallas_call(functools.partial(kernel, cfg), out_shape=(jax.ShapeDtypeS...  1.33 us
    unnamed x6, local copies, waits for them, and re-layouts  1.27 us

profile of v1, /device:TPU:0, one launch (start us, length us, event | category | flops | bytes accessed | tf_op | source)
XLA Modules:
  0.0 39.1 jit_solution(10966788947109556297)
XLA Ops:
  0.6 35.9 %tree_sweep.1 = (f32[1,4,1024]{2,1,0:T(4,128)}, f32[1,3,1024]{2,1,0:T(4,128)}, f32[1,1,1024]{2,1,0:T(1,128)}) custom-call(f32[1,4,1024]{2,1,0:T(4,128)} %leaf_ref.1, f32[3,8,1024]{2,1,0:T(8,128)} %local_ref.1, f32[1,8,1024]{2,1,0:T(8,128)} %top_ref.1), custom_call_target="tpu_custom_call" | custom-call | tf_op jit(solution)/shard_map/tree_sweep/pallas_call | solution.py:394
  36.5 0.0 copy-start
  36.5 1.3 %copy.6 = f32[1,3,1024]{2,0,1:T(1,128)} copy(f32[1,3,1024]{2,1,0:T(4,128)} %get-tuple-element.4) | data formatting | bytes 24576 | tf_op jit(solution)/shard_map/tree_sweep/pallas_call | solution.py:394
  37.8 0.0 copy-done
  37.8 0.0 copy-start.1
  37.9 0.6 %copy.9 = f32[1,4,1024]{2,1,0:T(4,128)} copy(f32[1,4,1024]{2,1,0:T(4,128)S(1)} %copy-done) | data formatting | bytes 32768
  38.5 0.1 copy-done.1
  38.5 0.6 %copy.10 = f32[1,1,1024]{2,1,0:T(1,128)} copy(f32[1,1,1024]{2,1,0:T(1,128)S(1)} %copy-done.1) | data formatting | bytes 8192
Async XLA Ops:
  36.5 1.3 %copy-start = (f32[1,4,1024]{2,1,0:T(4,128)S(1)}, f32[1,4,1024]{2,1,0:T(4,128)}, u32[]{:S(2)}) copy-start(f32[1,4,1024]{2,1,0:T(4,128)} %get-tuple-element.9) | copy-start | bytes 49156
  37.8 0.7 %copy-start.1 = (f32[1,1,1024]{2,1,0:T(1,128)S(1)}, f32[1,1,1024]{2,1,0:T(1,128)}, u32[]{:S(2)}) copy-start(f32[1,1,1024]{2,1,0:T(1,128)} %get-tuple-element.11) | copy-start | bytes 12292

commit v2 on v1

--- a/solution.py
+++ b/solution.py
@@ -51,7 +51,7 @@
     loc,
     wk,
     wm,
-    wrep,
+    wq,
     yt,
     fbuf,
     tbuf,
@@ -185,18 +185,35 @@
         lax.broadcasted_iota(jnp.int32, (chi, chunks), 0) // rep
         == lax.broadcasted_iota(jnp.int32, (chi, chunks), 1)
     ).astype(jnp.float32)
+    sub = chi // rep
     widen = (
-        lax.broadcasted_iota(jnp.int32, (LANES, cols), 1) // chi
-        == lax.rem(lax.broadcasted_iota(jnp.int32, (LANES, cols), 0), chi)
+        lax.broadcasted_iota(jnp.int32, (LANES, chi * sub), 1) // sub
+        == lax.rem(lax.broadcasted_iota(jnp.int32, (LANES, chi * sub), 0), chi)
     ).astype(jnp.float32).astype(jnp.bfloat16)
-    copy_row = lax.broadcasted_iota(jnp.int32, (2 * LANES, rep * LANES), 0)
-    copy_lane = lax.broadcasted_iota(jnp.int32, (2 * LANES, rep * LANES), 1)
-    copies = jnp.where(
-        (lax.rem(copy_row, LANES) // chi == copy_lane // LANES)
-        & (lax.rem(copy_row, chi) == lax.rem(copy_lane, chi)),
-        1.0,
-        0.0,
-    ).astype(jnp.bfloat16)
+    unit_mask = lax.rem(
+        lax.broadcasted_iota(jnp.int32, (sub, chi * sub), 1), sub
+    ) == lax.broadcasted_iota(jnp.int32, (sub, chi * sub), 0)
+    part_group = lax.broadcasted_iota(jnp.int32, (chunks * sub, LANES), 1) // chi
+
+    def swap_groups(value):
+        parts = [
+            jnp.concatenate(
+                [value[g * chi + v * sub : g * chi + (v + 1) * sub] for g in range(chunks)], axis=0
+            )
+            for v in range(rep)
+        ]
+        bit = 1
+        while bit < rep:
+            lower = lax.rem(part_group // bit, 2) == 0
+            for a in range(rep):
+                if a & bit == 0:
+                    one, two = parts[a], parts[a | bit]
+                    parts[a] = jnp.where(lower, one, pltpu.roll(two, bit * chi, 1))
+                    parts[a | bit] = jnp.where(lower, pltpu.roll(one, LANES - bit * chi, 1), two)
+            bit *= 2
+        return jnp.concatenate(
+            [parts[v][g * sub : (g + 1) * sub] for g in range(chunks) for v in range(rep)], axis=0
+        )
 
     def fold(value):
         shift = chi
@@ -244,12 +261,7 @@
         wm[item] = jnp.concatenate([high, low] * (rep // 2), axis=0)
         stack = jnp.concatenate([lanes_to_rows(high), lanes_to_rows(low)], axis=1)
         wk[item] = stack
-        spread_out = dot(stack, copies)
-        for g in range(chunks):
-            for i in range(rep):
-                wrep[item, rep * g + i] = spread_out[
-                    g * chi : (g + 1) * chi, i * LANES : (i + 1) * LANES
-                ]
+        wq[item] = jnp.concatenate(halves(swap_groups(lanes_to_rows(value))), axis=1)
 
     def act_minor(item, env):
         block = jnp.where(block_mask, jnp.concatenate([env] * rep, axis=0), 0.0)
@@ -263,18 +275,17 @@
         low = jnp.where(group == 2, rest - middle, 0.0)
         parts = jnp.where(group == 0, high, jnp.where(group == 1, middle, low))
         fbuf[...] = dot(parts.astype(jnp.bfloat16), widen)
-
-        def step(y, sums):
-            line = fbuf[pl.ds(y, 1), :]
-            block = wrep[item, y]
-            return tuple(
-                sums[g] + line[:, g * LANES : (g + 1) * LANES] * block for g in range(chunks)
-            )
-
-        zero = jnp.zeros((chi, LANES), jnp.float32)
-        sums = lax.fori_loop(0, chi, step, (zero,) * chunks, unroll=4)
-        yt[item] = jnp.concatenate(halves(jnp.concatenate(sums, axis=0).T), axis=0)
-        return jnp.concatenate(sums, axis=1)
+        wide = jnp.concatenate(
+            [
+                jnp.where(unit_mask, jnp.broadcast_to(fbuf[y : y + 1, :], unit_mask.shape), 0.0)
+                for y in range(chi)
+            ],
+            axis=0,
+        )
+        acted = dot(jnp.concatenate(halves(wide), axis=0), wq[item])
+        acted = swap_groups(join_lanes(join_rows(acted)))
+        yt[item] = jnp.concatenate(halves(acted.T), axis=0)
+        return rows_to_lanes(acted)
 
     def close(left, right):
         high, low = halves(right)
@@ -405,9 +416,9 @@
             pltpu.VMEM((bonds, nodes, share, cols), f32),
             pltpu.VMEM((items, cols * chi // LANES, 2 * LANES), jnp.bfloat16),
             pltpu.VMEM((items, LANES, cols), jnp.bfloat16),
-            pltpu.VMEM((items, chi, chi, LANES), f32),
+            pltpu.VMEM((items, cols * chi // LANES, 2 * LANES), jnp.bfloat16),
             pltpu.VMEM((items, 2 * LANES, cols * chi // LANES), jnp.bfloat16),
-            pltpu.VMEM((chi, cols), f32),
+            pltpu.VMEM((chi, cols * chi // LANES), f32),
             pltpu.VMEM((cols, chi), f32),
             pltpu.VMEM((levels, chi, LANES), f32),
             pltpu.VMEM((levels, chi, LANES), f32),

time: 39.4 us -> 36.7 us (0.931)
  Pallas kernels: 35.9 us -> 33.1 us
    pallas_call x1, Pallas kernels: 35.9 us -> 33.1 us  [body(): pl.pallas_call(functools.partial(kernel, cfg), out_shape=(jax.ShapeDtypeS...]
where the time goes in v2:
time: 36.7 us; the launch traced here: 36.4 us
  Pallas kernels  33.1 us (90%)
  local copies, waits for them, and re-layouts  2.61 us (7%)
  between operations  0.65 us (2%)
    pallas_call x1, Pallas kernels, body(): pl.pallas_call(functools.partial(kernel, cfg), out_shape=(jax.ShapeDtypeS...  33.1 us
    pallas_call x1, local copies, waits for them, and re-layouts, body(): pl.pallas_call(functools.partial(kernel, cfg), out_shape=(jax.ShapeDtypeS...  1.33 us
    unnamed x6, local copies, waits for them, and re-layouts  1.27 us

profile of v2, /device:TPU:0, one launch (start us, length us, event | category | flops | bytes accessed | tf_op | source)
XLA Modules:
  0.0 36.4 jit_solution(1260244301473823349)
XLA Ops:
  0.6 33.1 %tree_sweep.1 = (f32[1,4,1024]{2,1,0:T(4,128)}, f32[1,3,1024]{2,1,0:T(4,128)}, f32[1,1,1024]{2,1,0:T(1,128)}) custom-call(f32[1,4,1024]{2,1,0:T(4,128)} %leaf_ref.1, f32[3,8,1024]{2,1,0:T(8,128)} %local_ref.1, f32[1,8,1024]{2,1,0:T(8,128)} %top_ref.1), custom_call_target="tpu_custom_call" | custom-call | tf_op jit(solution)/shard_map/tree_sweep/pallas_call | solution.py:405
  33.8 0.0 copy-start
  33.8 1.3 %copy.6 = f32[1,3,1024]{2,0,1:T(1,128)} copy(f32[1,3,1024]{2,1,0:T(4,128)} %get-tuple-element.4) | data formatting | bytes 24576 | tf_op jit(solution)/shard_map/tree_sweep/pallas_call | solution.py:405
  35.1 0.0 copy-done
  35.1 0.0 copy-start.1
  35.1 0.6 %copy.9 = f32[1,4,1024]{2,1,0:T(4,128)} copy(f32[1,4,1024]{2,1,0:T(4,128)S(1)} %copy-done) | data formatting | bytes 32768
  35.7 0.1 copy-done.1
  35.8 0.6 %copy.10 = f32[1,1,1024]{2,1,0:T(1,128)} copy(f32[1,1,1024]{2,1,0:T(1,128)S(1)} %copy-done.1) | data formatting | bytes 8192
Async XLA Ops:
  33.8 1.3 %copy-start = (f32[1,4,1024]{2,1,0:T(4,128)S(1)}, f32[1,4,1024]{2,1,0:T(4,128)}, u32[]{:S(2)}) copy-start(f32[1,4,1024]{2,1,0:T(4,128)} %get-tuple-element.9) | copy-start | bytes 49156
  35.1 0.7 %copy-start.1 = (f32[1,1,1024]{2,1,0:T(1,128)S(1)}, f32[1,1,1024]{2,1,0:T(1,128)}, u32[]{:S(2)}) copy-start(f32[1,1,1024]{2,1,0:T(1,128)} %get-tuple-element.11) | copy-start | bytes 12292

commit v3 on v2

--- a/solution.py
+++ b/solution.py
@@ -232,10 +232,10 @@
         )
         return fold(jnp.where(row_mask, mm(spread, tile), 0.0))
 
-    def flatten(matrix, out, index):
+    def flatten(matrix, out, index, lead=0):
         tile = mm(pick, jnp.where(row_mask, matrix, 0.0))
         for g in range(chunks):
-            out[0, index : index + 1, g * LANES : (g + 1) * LANES] = tile[g : g + 1]
+            out[lead, index : index + 1, g * LANES : (g + 1) * LANES] = tile[g : g + 1]
 
     def lanes_to_rows(value):
         return jnp.concatenate(
@@ -308,8 +308,8 @@
     advance()
     for copy in local_moves[0]:
         copy.wait_recv()
-    waited = 1
     node = 0
+    late = []
     for height in range(1, height_dev + 1):
         if height == 2:
             for copy in local_moves[1]:
@@ -319,10 +319,9 @@
         for n in range(leaves >> height):
             value = jnp.concatenate([loc[j, node] for j in range(bonds)], axis=0)
             store(2 * node, value)
-            store(2 * node + 1, swap_children(value))
             left, right = current[2 * n], current[2 * n + 1]
             by_left = act_major(2 * node, left)
-            act_major(2 * node + 1, right)
+            late.append((node, right))
             grown.append(close(by_left, act_minor(2 * node, right)))
             node += 1
             advance()
@@ -364,11 +363,16 @@
         upper = lax.rem(position >> k, 2) == 1
         store(item, jnp.where(upper, value, swap_children(value)))
         minor = act_minor(item, env)
+        if k == levels - 1:
+            root = assemble(levels - 1, starts[levels], cols >> levels)
+            state = close(root, root)
+        for other, right in late[k::levels]:
+            value = jnp.concatenate([loc[j, other] for j in range(bonds)], axis=0)
+            store(2 * other + 1, swap_children(value))
+            act_major(2 * other + 1, right)
         copy.wait_recv()
         env = close(act_major(item, erecv[k]), minor)
 
-    root = assemble(levels - 1, starts[levels], cols >> levels)
-    state = close(root, root)
     top = env
     for k in range(levels - 1, -1, -1):
         marked = lax.rem(position + 1, 2 << k) == 1 << k
@@ -382,7 +386,7 @@
         below = []
         for n in range(count):
             node = offset + n
-            flatten(states[n], inner_out, node)
+            flatten(states[n], inner_out, 0, node)
             below.append(descend(2 * node + 1, states[n]))
             below.append(descend(2 * node, states[n]))
         states = below
@@ -402,11 +406,11 @@
     f32 = jnp.float32
     dma = pltpu.SemaphoreType.DMA
     vmem = pl.BlockSpec(memory_space=pltpu.VMEM)
-    return pl.pallas_call(
+    leaf_rho, inner_rho, top_rho = pl.pallas_call(
         functools.partial(kernel, cfg),
         out_shape=(
             jax.ShapeDtypeStruct((1, leaves, cols), f32),
-            jax.ShapeDtypeStruct((1, nodes, cols), f32),
+            jax.ShapeDtypeStruct((nodes, 1, cols), f32),
             jax.ShapeDtypeStruct((1, 1, cols), f32),
         ),
         in_specs=[vmem] * 3,
@@ -435,6 +439,7 @@
         compiler_params=pltpu.CompilerParams(collective_id=0, has_side_effects=True),
         name="tree_sweep",
     )(leaf_metric, local_iso, top_iso)
+    return leaf_rho, inner_rho.transpose(1, 0, 2), top_rho
 
 
 def solution(mesh):

time: 36.7 us -> 35.2 us (0.959)
  Pallas kernels: 33.1 us -> 31.6 us
    pallas_call x1, Pallas kernels: 33.1 us -> 31.6 us  [body(): pl.pallas_call(functools.partial(kernel, cfg), out_shape=(jax.ShapeDtypeS...]
    pallas_call x1 -> x0, local copies, waits for them, and re-layouts: 1.33 us -> none  [body(): pl.pallas_call(functools.partial(kernel, cfg), out_shape=(jax.ShapeDtypeS...]
    unnamed x6 -> x7, local copies, waits for them, and re-layouts: 1.27 us -> 2.6 us
where the time goes in v3:
time: 35.2 us; the launch traced here: 34.9 us
  Pallas kernels  31.6 us (90%)
  local copies, waits for them, and re-layouts  2.6 us (7%)
  between operations  0.65 us (2%)
    pallas_call x1, Pallas kernels, body(): pl.pallas_call(functools.partial(kernel, cfg), out_shape=(jax.ShapeDtypeS...  31.6 us
    unnamed x7, local copies, waits for them, and re-layouts  2.6 us

profile of v3, /device:TPU:0, one launch (start us, length us, event | category | flops | bytes accessed | tf_op | source)
XLA Modules:
  0.0 34.9 jit_solution(14002978045708755915)
XLA Ops:
  0.6 31.6 %tree_sweep.1 = (f32[1,4,1024]{2,1,0:T(4,128)}, f32[3,1,1024]{2,1,0:T(1,128)}, f32[1,1,1024]{2,1,0:T(1,128)}) custom-call(f32[1,4,1024]{2,1,0:T(4,128)} %leaf_ref.1, f32[3,8,1024]{2,1,0:T(8,128)} %local_ref.1, f32[1,8,1024]{2,1,0:T(8,128)} %top_ref.1), custom_call_target="tpu_custom_call" | custom-call | tf_op jit(solution)/shard_map/tree_sweep/pallas_call | solution.py:409
  32.2 0.0 copy-start
  32.3 1.3 %copy.9 = f32[1,4,1024]{2,1,0:T(4,128)} copy(f32[1,4,1024]{2,1,0:T(4,128)} %get-tuple-element.12) | data formatting | bytes 32768
  33.6 0.0 copy-done
  33.6 0.0 copy-start.1
  33.6 0.6 %copy.10 = f32[1,3,1024]{2,0,1:T(1,128)} copy(f32[1,3,1024]{2,0,1:T(1,128)S(1)} %bitcast.1) | data formatting | bytes 24576
  34.2 0.1 copy-done.1
  34.3 0.6 %copy.11 = f32[1,1,1024]{2,1,0:T(1,128)} copy(f32[1,1,1024]{2,1,0:T(1,128)S(1)} %copy-done.1) | data formatting | bytes 8192
Async XLA Ops:
  32.2 1.3 %copy-start = (f32[3,1,1024]{2,1,0:T(1,128)S(1)}, f32[3,1,1024]{2,1,0:T(1,128)}, u32[]{:S(2)}) copy-start(f32[3,1,1024]{2,1,0:T(1,128)} %get-tuple-element.7) | copy-start | bytes 36868
  33.6 0.7 %copy-start.1 = (f32[1,1,1024]{2,1,0:T(1,128)S(1)}, f32[1,1,1024]{2,1,0:T(1,128)}, u32[]{:S(2)}) copy-start(f32[1,1,1024]{2,1,0:T(1,128)} %get-tuple-element.14) | copy-start | bytes 12292

commit v4 on v3

--- a/solution.py
+++ b/solution.py
@@ -74,7 +74,6 @@
     levels = devices.bit_length() - 1
     height_dev = leaves.bit_length() - 1
     nodes = leaves - 1
-    first = leaves // 2
     position = lax.axis_index("leaf")
     mine = lax.axis_index("bond")
 
@@ -153,10 +152,10 @@
         sends.extend(found)
         return found
 
-    local_moves = [local_copies(0, 0, first)]
+    local_moves = [local_copies(0, 0, 1)]
     leaf_moves = [leaf_copy(0)]
-    if nodes > first:
-        local_moves.append(local_copies(1, first, nodes))
+    for n in range(1, nodes):
+        local_moves.append(local_copies(n, n, n + 1))
     forward_moves = []
     for copy in own:
         copy.wait()
@@ -306,17 +305,14 @@
 
     envs = [[unflatten(leaf_ref[0, n : n + 1, :]) for n in range(leaves)]]
     advance()
-    for copy in local_moves[0]:
-        copy.wait_recv()
     node = 0
     late = []
     for height in range(1, height_dev + 1):
-        if height == 2:
-            for copy in local_moves[1]:
-                copy.wait_recv()
         current = envs[-1]
         grown = []
         for n in range(leaves >> height):
+            for copy in local_moves[node]:
+                copy.wait_recv()
             value = jnp.concatenate([loc[j, node] for j in range(bonds)], axis=0)
             store(2 * node, value)
             left, right = current[2 * n], current[2 * n + 1]
@@ -427,8 +423,8 @@
             pltpu.VMEM((levels, chi, LANES), f32),
             pltpu.VMEM((levels, chi, LANES), f32),
             dma((2,)),
-            dma((2, bonds - 1)),
-            dma((2, bonds - 1)),
+            dma((nodes, bonds - 1)),
+            dma((nodes, bonds - 1)),
             dma((levels,)),
             dma((levels,)),
             dma((levels, bonds - 1)),

time: 35.2 us -> 35 us (level)
  no operation moved by 1% of the time
where the time goes in v4:
time: 35 us; the launch traced here: 34.7 us
  Pallas kernels  31.5 us (90%)
  local copies, waits for them, and re-layouts  2.6 us (7%)
  between operations  0.65 us (2%)
    pallas_call x1, Pallas kernels, body(): pl.pallas_call(functools.partial(kernel, cfg), out_shape=(jax.ShapeDtypeS...  31.5 us
    unnamed x7, local copies, waits for them, and re-layouts  2.6 us

profile of v4, /device:TPU:0, one launch (start us, length us, event | category | flops | bytes accessed | tf_op | source)
XLA Modules:
  0.0 34.7 jit_solution(4915520174348356154)
XLA Ops:
  0.6 31.5 %tree_sweep.1 = (f32[1,4,1024]{2,1,0:T(4,128)}, f32[3,1,1024]{2,1,0:T(1,128)}, f32[1,1,1024]{2,1,0:T(1,128)}) custom-call(f32[1,4,1024]{2,1,0:T(4,128)} %leaf_ref.1, f32[3,8,1024]{2,1,0:T(8,128)} %local_ref.1, f32[1,8,1024]{2,1,0:T(8,128)} %top_ref.1), custom_call_target="tpu_custom_call" | custom-call | tf_op jit(solution)/shard_map/tree_sweep/pallas_call | solution.py:405
  32.1 0.0 copy-start
  32.1 1.3 %copy.9 = f32[1,4,1024]{2,1,0:T(4,128)} copy(f32[1,4,1024]{2,1,0:T(4,128)} %get-tuple-element.12) | data formatting | bytes 32768
  33.5 0.0 copy-done
  33.5 0.0 copy-start.1
  33.5 0.6 %copy.10 = f32[1,3,1024]{2,0,1:T(1,128)} copy(f32[1,3,1024]{2,0,1:T(1,128)S(1)} %bitcast.1) | data formatting | bytes 24576
  34.1 0.1 copy-done.1
  34.1 0.6 %copy.11 = f32[1,1,1024]{2,1,0:T(1,128)} copy(f32[1,1,1024]{2,1,0:T(1,128)S(1)} %copy-done.1) | data formatting | bytes 8192
Async XLA Ops:
  32.1 1.3 %copy-start = (f32[3,1,1024]{2,1,0:T(1,128)S(1)}, f32[3,1,1024]{2,1,0:T(1,128)}, u32[]{:S(2)}) copy-start(f32[3,1,1024]{2,1,0:T(1,128)} %get-tuple-element.7) | copy-start | bytes 36868
  33.5 0.7 %copy-start.1 = (f32[1,1,1024]{2,1,0:T(1,128)S(1)}, f32[1,1,1024]{2,1,0:T(1,128)}, u32[]{:S(2)}) copy-start(f32[1,1,1024]{2,1,0:T(1,128)} %get-tuple-element.14) | copy-start | bytes 12292
